TPU v7x, 32 devices: a whole 2x2x4 slice. The times are simulated.
32 devices in a mesh: dp: 8 (over z, y), mix: 4 (over x, core).
Axes of the slice: x: 2, y: 2, z: 4, core: 2. Of those that a mesh axis runs over, the one named last changes fastest.
Arguments:
- patches: bfloat16 [224, 196, 768], P('dp', 'mix'), may hold values from -6 to 6
- valid_counts: int32 [8], P('dp'), may hold values from 7 to 28, as said below
- gain_one: float32 [768], replicated, may hold values from 0.5 to 1.5
- shift_one: float32 [768], replicated, may hold values from -1.25 to 1.25
- tok_in: bfloat16 [196, 384], replicated, may hold values from -0.4375 to 0.4375
- tok_inbias: float32 [384], replicated, may hold values from -1.25 to 1.25
- tok_out: bfloat16 [384, 196], replicated, may hold values from -0.3125 to 0.3125
- tok_outbias: float32 [196], replicated, may hold values from -1.25 to 1.25
- gain_two: float32 [768], replicated, may hold values from 0.5 to 1.5
- shift_two: float32 [768], replicated, may hold values from -1.25 to 1.25
- chan_in: bfloat16 [768, 3072], replicated, may hold values from -0.21875 to 0.21875
- chan_inbias: float32 [3072], replicated, may hold values from -1.25 to 1.25
- chan_out: bfloat16 [3072, 768], replicated, may hold values from -0.109375 to 0.109375
- chan_outbias: float32 [768], replicated, may hold values from -1.25 to 1.25
- out_grad: bfloat16 [224, 196, 768], P('dp', 'mix'), may hold values from -6 to 6
Outputs:
- mixed_out: bfloat16 [224, 196, 768], P('dp', 'mix')
- patch_grad: bfloat16 [224, 196, 768], P('dp', 'mix')
- grad_gain_one: float32 [768], replicated
- grad_shift_one: float32 [768], replicated
- grad_tok_in: float32 [196, 384], replicated
- grad_tok_inbias: float32 [384], replicated
- grad_tok_out: float32 [384, 196], replicated
- grad_tok_outbias: float32 [196], replicated
- grad_gain_two: float32 [768], replicated
- grad_shift_two: float32 [768], replicated
- grad_chan_in: float32 [768, 3072], replicated
- grad_chan_inbias: float32 [3072], replicated
- grad_chan_out: float32 [3072, 768], replicated
- grad_chan_outbias: float32 [768], replicated
Inputs may be any that keep to these rules, and one draw needn't show every extreme that they name: `valid_counts`: how many of the 28 images of each index of dp are real; the rest are padding and get no gradient.
All inputs are finite; a program needn't handle non-finite values.
Results may differ from a plain program's by a relative error of at most 0.008.
Values may be sent and summed in bfloat16 or wider, within the bound.
A program may use at most 192 MiB of HBM per device.

v0:
```python
import jax
import jax.numpy as jnp
from jax import lax
from jax.sharding import PartitionSpec as P

EPS = 1e-06


def layer_norm(values, gain, shift):
    center = values - jnp.mean(values, axis=-1, keepdims=True)
    spread = jnp.mean(center * center, axis=-1, keepdims=True)
    return center * lax.rsqrt(spread + EPS) * gain + shift


def shards(
    patches,
    valid_counts,
    gain_one,
    shift_one,
    tok_in,
    tok_inbias,
    tok_out,
    tok_outbias,
    gain_two,
    shift_two,
    chan_in,
    chan_inbias,
    chan_out,
    chan_outbias,
    out_grad,
):
    images, part, width = patches.shape
    rowcount = images * part
    inputs = patches.astype(jnp.float32)
    normed_full, first_back = jax.vjp(layer_norm, inputs, gain_one, shift_one)
    normed = normed_full.astype(jnp.bfloat16)
    columns = lax.all_to_all(normed, "mix", split_axis=2, concat_axis=1, tiled=True)
    widened = (
        jnp.einsum("bsc,sk->bkc", columns, tok_in, preferred_element_type=jnp.float32)
        + tok_inbias[None, :, None]
    )
    hidden = jax.nn.gelu(widened).astype(jnp.bfloat16)
    mixed_cols = (
        jnp.einsum("bkc,ks->bsc", hidden, tok_out, preferred_element_type=jnp.float32)
        + tok_outbias[None, :, None]
    ).astype(jnp.bfloat16)
    mixed = lax.all_to_all(mixed_cols, "mix", split_axis=1, concat_axis=2, tiled=True)
    middle = inputs + mixed.astype(jnp.float32)
    second_full, second_back = jax.vjp(layer_norm, middle, gain_two, shift_two)
    second = second_full.astype(jnp.bfloat16).reshape(rowcount, width)
    inner = jnp.dot(second, chan_in, preferred_element_type=jnp.float32) + chan_inbias
    activ = jax.nn.gelu(inner).astype(jnp.bfloat16)
    branch = jnp.dot(activ, chan_out, preferred_element_type=jnp.float32) + chan_outbias
    mixed_out = (middle + branch.reshape(images, part, width)).astype(jnp.bfloat16)
    live = jnp.arange(images, dtype=jnp.int32) < valid_counts[0]
    upstream = jnp.where(live[:, None, None], out_grad, jnp.zeros_like(out_grad)).reshape(
        rowcount, width
    )
    inner_again = jnp.dot(second, chan_in, preferred_element_type=jnp.float32) + chan_inbias
    activ_full, chan_gelu_back = jax.vjp(jax.nn.gelu, inner_again)
    activ_again = activ_full.astype(jnp.bfloat16)
    grad_chan_out = jnp.einsum(
        "rf,rc->fc", activ_again, upstream, preferred_element_type=jnp.float32
    )
    grad_chan_outbias = jnp.sum(upstream.astype(jnp.float32), axis=0)
    grad_activ = jnp.einsum("rc,fc->rf", upstream, chan_out, preferred_element_type=jnp.float32)
    grad_inner = chan_gelu_back(grad_activ)[0].astype(jnp.bfloat16)
    grad_chan_in = jnp.einsum("rc,rf->cf", second, grad_inner, preferred_element_type=jnp.float32)
    grad_chan_inbias = jnp.sum(grad_inner.astype(jnp.float32), axis=0)
    grad_second = jnp.einsum("rf,cf->rc", grad_inner, chan_in, preferred_element_type=jnp.float32)
    grad_middle, grad_gain_two, grad_shift_two = second_back(
        grad_second.reshape(images, part, width)
    )
    grad_middle = grad_middle + upstream.astype(jnp.float32).reshape(images, part, width)
    grad_cols = lax.all_to_all(
        grad_middle.astype(jnp.bfloat16), "mix", split_axis=2, concat_axis=1, tiled=True
    )
    widened_again = (
        jnp.einsum("bsc,sk->bkc", columns, tok_in, preferred_element_type=jnp.float32)
        + tok_inbias[None, :, None]
    )
    hidden_full, tok_gelu_back = jax.vjp(jax.nn.gelu, widened_again)
    hidden_again = hidden_full.astype(jnp.bfloat16)
    grad_tok_out = jnp.einsum(
        "bkc,bsc->ks", hidden_again, grad_cols, preferred_element_type=jnp.float32
    )
    grad_tok_outbias = jnp.sum(grad_cols.astype(jnp.float32), axis=(0, 2))
    grad_hidden = jnp.einsum("ks,bsc->bkc", tok_out, grad_cols, preferred_element_type=jnp.float32)
    grad_widened = tok_gelu_back(grad_hidden)[0].astype(jnp.bfloat16)
    grad_tok_in = jnp.einsum(
        "bsc,bkc->sk", columns, grad_widened, preferred_element_type=jnp.float32
    )
    grad_tok_inbias = jnp.sum(grad_widened.astype(jnp.float32), axis=(0, 2))
    grad_columns = jnp.einsum(
        "sk,bkc->bsc", tok_in, grad_widened, preferred_element_type=jnp.float32
    ).astype(jnp.bfloat16)
    grad_normed = lax.all_to_all(grad_columns, "mix", split_axis=1, concat_axis=2, tiled=True)
    grad_inputs, grad_gain_one, grad_shift_one = first_back(grad_normed.astype(jnp.float32))
    patch_grad = (grad_middle + grad_inputs).astype(jnp.bfloat16)
    summed = lax.psum(
        (
            grad_gain_one,
            grad_shift_one,
            grad_tok_in,
            grad_tok_inbias,
            grad_tok_out,
            grad_tok_outbias,
            grad_gain_two,
            grad_shift_two,
            grad_chan_in,
            grad_chan_inbias,
            grad_chan_out,
            grad_chan_outbias,
        ),
        ("dp", "mix"),
    )
    return (
        mixed_out,
        patch_grad,
        summed[0],
        summed[1],
        summed[2],
        summed[3],
        summed[4],
        summed[5],
        summed[6],
        summed[7],
        summed[8],
        summed[9],
        summed[10],
        summed[11],
    )


def solution(mesh):
    return jax.shard_map(
        shards,
        mesh=mesh,
        in_specs=(
            P("dp", "mix", None),
            P("dp"),
            P(),
            P(),
            P(),
            P(),
            P(),
            P(),
            P(),
            P(),
            P(),
            P(),
            P(),
            P(),
            P("dp", "mix", None),
        ),
        out_specs=(
            P("dp", "mix", None),
            P("dp", "mix", None),
            P(),
            P(),
            P(),
            P(),
            P(),
            P(),
            P(),
            P(),
            P(),
            P(),
            P(),
            P(),
        ),
        check_vma=False,
    )
```

profile of v0, /device:TPU:0, one launch (start us, length us, event | category | flops | bytes accessed | tf_op | source)
XLA Modules:
  0.0 723.8 jit_solution(6114710992727440725)
XLA Ops:
  15.3 11.4 %copy.67 = bf16[28,49,768]{1,0,2:T(8,128)(2,1)} copy(bf16[28,49,768]{2,1,0:T(8,128)(2,1)} %fusion.25) | data formatting | bytes 4214784 | tf_op jit(solution)/shard_map/convert_element_type | solution.py:36
  26.7 11.5 %reshape.138 = bf16[4,2,131712]{2,1,0:T(2,128)(2,1)} reshape(bf16[768,28,49]{2,1,0:T(8,128)(2,1)} %bitcast.86) | data formatting | bytes 4214784
  38.2 31.3 %all_to_all.54 = bf16[4,2,131712]{2,1,0:T(2,128)(2,1)} all-to-all(bf16[4,2,131712]{2,1,0:T(2,128)(2,1)} %reshape.138), channel_id=1, replica_groups=mesh['dp'=8,'mix'=4] {'mix'}, dimensions={0} | all-to-all | bytes 4214784 | tf_op jit(solution)/shard_map/all_to_all | solution.py:37
  69.6 11.9 %reshape.139 = bf16[768,28,49]{2,1,0:T(8,128)(2,1)} reshape(bf16[4,2,131712]{2,1,0:T(2,128)(2,1)} %all_to_all.54) | data formatting | bytes 4214784
  81.5 9.6 %copy.68 = bf16[28,49,4,192]{3,1,2,0:T(8,128)(2,1)} copy(bf16[28,49,4,192]{1,0,3,2:T(8,128)(2,1)} %bitcast.84) | data formatting | bytes 4214784 | tf_op jit(solution)/shard_map/all_to_all | solution.py:37
  96.8 7.8 %fusion.17 = (bf16[28,384,192]{1,2,0:T(8,128)(2,1)S(1)}, f32[28,192,384]{2,1,0:T(8,128)}) fusion(f32[384]{0:T(512)S(1)} %copy-done.29, bf16[28,196,192]{2,1,0:T(8,128)(2,1)} %all_to_all.43, bf16[196,384]{1,0:T(8,128)(2,1)S(1)} %copy-done), kind=kOutput, calls=%fused_computation.26 | convolution fusion | flops 829882368 | bytes 14645760 | tf_op jit(solution)/shard_map/bsc,sk->bkc/dot_general | solution.py:39
  109.7 7.4 %copy.70 = bf16[28,196,192]{2,0,1:T(8,128)(2,1)} copy(bf16[28,196,192]{1,2,0:T(8,128)(2,1)} %fusion.30) | data formatting | bytes 4214784 | tf_op jit(solution)/shard_map/convert_element_type | solution.py:46
  131.1 28.5 %all-to-all-done.1 = bf16[28,196,192]{2,0,1:T(8,128)(2,1)} async-done(((bf16[28,196,192]{2,0,1:T(8,128)(2,1)}), bf16[28,196,192]{2,0,1:T(8,128)(2,1)}, u32[]{:S(2)}, u32[]{:S(2)}) %all-to-all-start.1) | async-done | bytes 2107424 | tf_op jit(solution)/shard_map/all_to_all | solution.py:47
  159.6 7.5 %copy.71 = bf16[28,196,192]{1,2,0:T(8,128)(2,1)} copy(bf16[28,196,192]{2,0,1:T(8,128)(2,1)} %all-to-all-done.1) | data formatting | bytes 4214784 | tf_op jit(solution)/shard_map/all_to_all | solution.py:47
  179.2 7.5 %copy.73 = f32[28,49,4,192]{3,2,1,0:T(4,128)} copy(f32[28,49,4,192]{3,1,2,0:T(8,128)} %bitcast.82) | data formatting | bytes 8429568 | tf_op jit(solution)/shard_map/convert_element_type | solution.py:48
  186.6 7.7 %reshape.130 = f32[28,49,768]{2,1,0:T(8,128)} reshape(f32[28,49,4,192]{3,2,1,0:T(4,128)} %copy.73) | data formatting | bytes 8429568 | tf_op jit(solution)/shard_map/convert_element_type | solution.py:48
  202.4 17.7 %multiply_convert_fusion = (bf16[1372,3072]{1,0:T(8,128)(2,1)}, f32[1372,3072]{1,0:T(8,128)}) fusion(f32[3072]{0:T(1024)S(1)} %copy-done.27, bf16[1372,768]{1,0:T(8,128)(2,1)} %reshape.126, bf16[768,3072]{1,0:T(8,128)(2,1)} %param.25), kind=kOutput, calls=%fused_computation.10 | convolution fusion | flops 6516056064 | bytes 32126976 | tf_op jit(solution)/shard_map/dot_general | solution.py:51
  220.2 19.9 %convert_reduce_fusion = (f32[3072]{0:T(1024)S(1)}, bf16[1372,3072]{1,0:T(8,128)(2,1)S(1)}) fusion(f32[1372,3072]{1,0:T(8,128)} %get-tuple-element.40, f32[3072]{0:T(1024)S(1)} %copy-done.27, bf16[1372,768]{1,0:T(8,128)(2,1)S(1)} %copy-done.11, bf16[3072,768]{1,0:T(8,128)(2,1)} %param.27), kind=kOutput, calls=%fused_computation.9 | convolution fusion | flops 6570845184 | bytes 32139264 | tf_op jit(solution)/shard_map/rc,fc->rf/dot_general | solution.py:66
  240.1 8.3 %fusion.41 = (f32[768]{0:T(1024)S(1)}, f32[1372,768]{1,0:T(8,128)}) fusion(bf16[1372,3072]{1,0:T(8,128)(2,1)S(1)} %get-tuple-element.46, bf16[768,3072]{1,0:T(8,128)(2,1)S(1)} %bitcast.92), kind=kOutput, calls=%fused_computation.81 | convolution fusion | flops 6474960896 | bytes 17366016 | tf_op jit(solution)/shard_map/rf,cf->rc/dot_general | solution.py:70
  258.3 12.2 %convolution_add_fusion = f32[1372,768]{1,0:T(8,128)} fusion(bf16[1372,3072]{1,0:T(8,128)(2,1)} %get-tuple-element.39, bf16[3072,768]{1,0:T(8,128)(2,1)} %param.27, f32[768]{0:T(1024)S(1)} %copy-done.28), kind=kOutput, calls=%fused_computation.54 | convolution fusion | flops 6474961920 | bytes 17366016 | tf_op jit(solution)/shard_map/dot_general | solution.py:53
  275.8 7.4 %fusion.39 = (f32[28,49]{1,0:T(8,128)S(1)}, f32[28,49,768]{2,1,0:T(8,128)S(1)}, bf16[28,49,768]{2,1,0:T(8,128)(2,1)}) fusion(f32[28,49]{1,0:T(8,128)S(1)} %multiply_multiply_fusion.5, f32[28,49,768]{2,1,0:T(8,128)} %copy-done.1, f32[28,49]{1,0:T(8,128)S(1)} %broadcast_multiply_fusion, f32[28,49]{1,0:T(8,128)S(1)} %fusion.38, f32[28,49,768]{2,1,0:T(8,128)} %reshape.129, ...), kind=kLoop, calls=%fused_computation.79 | loop fusion | flops 9481892 | bytes 18991552 | tf_op jit(solution)/shard_map/transpose(jvp())/reduce_sum | solution.py:10
  285.9 10.8 %copy.74 = bf16[28,49,768]{1,0,2:T(8,128)(2,1)} copy(bf16[28,49,768]{2,1,0:T(8,128)(2,1)S(1)} %fusion.29) | data formatting | bytes 4214784 | tf_op jit(solution)/shard_map/convert_element_type | solution.py:76
  296.8 11.5 %reshape.140 = bf16[4,2,131712]{2,1,0:T(2,128)(2,1)} reshape(bf16[768,28,49]{2,1,0:T(8,128)(2,1)} %bitcast.87) | data formatting | bytes 4214784
  312.0 13.2 %fusion.43 = f32[3072,768]{1,0:T(8,128)} fusion(bf16[1372,3072]{1,0:T(8,128)(2,1)} %get-tuple-element.39, bf16[1372,768]{1,0:T(8,128)(2,1)} %reshape.128), kind=kOutput, calls=%fused_computation.83 | convolution fusion | flops 6473908224 | bytes 19974144 | tf_op jit(solution)/shard_map/rf,rc->fc/dot_general | solution.py:62
  325.1 12.2 %fusion.42 = f32[768,3072]{1,0:T(8,128)} fusion(bf16[1372,768]{1,0:T(8,128)(2,1)S(1)} %copy-done.12, bf16[1372,3072]{1,0:T(8,128)(2,1)} %copy-done.33), kind=kOutput, calls=%fused_computation.82 | convolution fusion | flops 6473908224 | bytes 19974144 | tf_op jit(solution)/shard_map/rc,rf->cf/dot_general | solution.py:68
  337.7 10.9 %reshape.141 = bf16[768,28,49]{2,1,0:T(8,128)(2,1)} reshape(bf16[4,2,131712]{2,1,0:T(2,128)(2,1)S(1)} %all-to-all-done.2) | data formatting | bytes 4214784
  348.6 8.6 %copy.75 = bf16[28,49,4,192]{3,1,2,0:T(8,128)(2,1)S(1)} copy(bf16[28,49,4,192]{1,0,3,2:T(8,128)(2,1)} %bitcast.85) | data formatting | bytes 4214784 | tf_op jit(solution)/shard_map/all_to_all | solution.py:75
  365.4 9.6 %convert_reduce_fusion.1 = (f32[384]{0:T(512)S(1)}, bf16[28,384,192]{1,2,0:T(8,128)(2,1)S(1)}) fusion(f32[28,192,384]{2,1,0:T(8,128)} %get-tuple-element.38, f32[384]{0:T(512)S(1)} %copy-done.30, bf16[28,196,192]{2,1,0:T(8,128)(2,1)S(1)} %copy-done.10, bf16[384,196]{0,1:T(8,128)(2,1)S(1)} %copy-done.26), kind=kOutput, calls=%fused_computation.27 | convolution fusion | flops 856718976 | bytes 14647296 | tf_op jit(solution)/shard_map/ks,bsc->bkc/dot_general | solution.py:88
  384.6 7.5 %copy.77 = bf16[28,196,192]{2,0,1:T(8,128)(2,1)} copy(bf16[28,196,192]{1,2,0:T(8,128)(2,1)} %convert_bitcast_fusion) | data formatting | bytes 4214784 | tf_op jit(solution)/shard_map/convert_element_type | solution.py:96
  397.5 55.4 %all-to-all-done.3 = bf16[28,196,192]{2,0,1:T(8,128)(2,1)} async-done(((bf16[28,196,192]{2,0,1:T(8,128)(2,1)}), bf16[28,196,192]{2,0,1:T(8,128)(2,1)}, u32[]{:S(2)}, u32[]{:S(2)}) %all-to-all-start.3) | async-done | bytes 2107424 | tf_op jit(solution)/shard_map/all_to_all | solution.py:97
  452.9 7.0 copy.78
  463.7 7.0 reshape.133
  470.7 7.5 %copy.80 = f32[28,49,4,192]{3,2,1,0:T(4,128)} copy(f32[28,49,4,192]{3,1,2,0:T(8,128)} %bitcast.83) | data formatting | bytes 8429568 | tf_op jit(solution)/shard_map/convert_element_type | solution.py:98
  478.2 8.0 %reshape.131 = f32[28,49,768]{2,1,0:T(8,128)} reshape(f32[28,49,4,192]{3,2,1,0:T(4,128)} %copy.80) | data formatting | bytes 8429568 | tf_op jit(solution)/shard_map/convert_element_type | solution.py:98
  496.2 42.5 %all-reduce = (f32[768]{0:T(1024)}, f32[768]{0:T(1024)}, f32[384]{0:T(512)}, f32[196]{0:T(256)}, f32[768]{0:T(1024)}, /*index=5*/f32[768]{0:T(1024)}, f32[3072]{0:T(1024)}, f32[768]{0:T(1024)}) all-reduce(f32[768]{0:T(1024)S(1)} %get-tuple-element.16, f32[768]{0:T(1024)S(1)} %reduce_sum.199, ...), channel_id=1, replica_groups=mesh['dp'=8,'mix'=4] {'dp','mix'}, use_global_device_ids=true, to_apply=%region_9.10 | all-reduce | flops 7492 | bytes 59936 | tf_op jit(solution)/shard_map/psum | solution.py:100
  545.4 155.2 %all-reduce.4.cloned.1.call-done = (f32[196,384]{1,0:T(8,128)}, f32[384,196]{0,1:T(8,128)}, f32[768,3072]{1,0:T(8,128)}, f32[3072,768]{1,0:T(8,128)}) async-done(((f32[196,384]{1,0:T(8,128)}, f32[384,196]{0,1:T(8,128)}, f32[768,3072]{1,0:T(8,128)}, f32[3072,768]{1,0:T(8,128)}), (f32[196,384]{1,0:T(8,128)}, f32[384,196]{0,1:T(8,128)}, f32[768,3072]{1,0:T(8,128)}, ...) | async-done | bytes 19476496 | tf_op jit(solution)/shard_map/psum | solution.py:100
  704.2 8.8 %copy.95 = f32[768,3072]{1,0:T(8,128)} copy(f32[768,3072]{1,0:T(8,128)} %get-tuple-element.57) | data formatting | bytes 18874368
  (130 shorter events, 125.1 us)
Async XLA Ops:
  7.2 89.6 %copy-start = (bf16[196,384]{1,0:T(8,128)(2,1)S(1)}, bf16[196,384]{1,0:T(8,128)(2,1)}, u32[]{:S(2)}) copy-start(bf16[196,384]{1,0:T(8,128)(2,1)} %param.19) | copy-start | bytes 451588
  7.2 6.0 copy-start.2
  7.2 6.0 copy-start.19
  7.2 6.0 copy-start.23
  91.1 5.7 copy-start.29
  96.8 9.8 %copy-start.25 = (bf16[384,196]{0,1:T(8,128)(2,1)S(1)}, bf16[384,196]{0,1:T(8,128)(2,1)}, u32[]{:S(2)}) copy-start(bf16[384,196]{0,1:T(8,128)(2,1)} %param.21) | copy-start | bytes 451588
  96.8 9.8 %copy-start.31 = (f32[196]{0:T(256)S(1)}, f32[196]{0:T(256)}, u32[]{:S(2)}) copy-start(f32[196]{0:T(256)} %param.22) | copy-start | bytes 2356
  117.1 42.5 %all-to-all-start.1 = ((bf16[28,196,192]{2,0,1:T(8,128)(2,1)}), bf16[28,196,192]{2,0,1:T(8,128)(2,1)}, u32[]{:S(2)}, u32[]{:S(2)}) async-start(bf16[28,196,192]{2,0,1:T(8,128)(2,1)} %copy.70), calls=%async_computation.1 | async-start | bytes 6422528 | tf_op jit(solution)/shard_map/all_to_all | solution.py:47
  202.4 17.7 %copy-start.11 = (bf16[1372,768]{1,0:T(8,128)(2,1)S(1)}, bf16[1372,768]{1,0:T(8,128)(2,1)}, u32[]{:S(2)}) copy-start(bf16[1372,768]{1,0:T(8,128)(2,1)} %reshape.128) | copy-start | bytes 6322180
  202.4 37.7 %slice-start.3 = ((s8[4718592]{0:T(1024)(128)(4,1)}), s8[4194304]{0:T(1024)(128)(4,1)S(1)}, s32[]{:S(2)}) async-start(s8[4718592]{0:T(1024)(128)(4,1)} %bitcast.91), calls=%async_computation.8 | async-start | bytes 8388608
  220.2 20.0 %slice-start.4 = ((s8[4718592]{0:T(1024)(128)(4,1)}), s8[524288]{0:T(1024)(128)(4,1)S(1)}, s32[]{:S(2)}) async-start(s8[4718592]{0:T(1024)(128)(4,1)} %bitcast.91), calls=%async_computation.9 | async-start | bytes 1048576
  240.1 8.4 %copy-start.33 = (bf16[1372,3072]{1,0:T(8,128)(2,1)}, bf16[1372,3072]{1,0:T(8,128)(2,1)S(1)}, u32[]{:S(2)}) copy-start(bf16[1372,3072]{1,0:T(8,128)(2,1)S(1)} %get-tuple-element.46) | copy-start | bytes 25288708
  253.6 4.7 copy-start.28
  275.8 9.6 %copy-start.6 = (bf16[28,49,768]{2,1,0:T(8,128)(2,1)S(1)}, bf16[28,49,768]{2,1,0:T(8,128)(2,1)}, u32[]{:S(2)}) copy-start(bf16[28,49,768]{2,1,0:T(8,128)(2,1)} %get-tuple-element.31) | copy-start | bytes 6322180
  308.3 29.4 %all-to-all-start.2 = ((bf16[4,2,131712]{2,1,0:T(2,128)(2,1)}), bf16[4,2,131712]{2,1,0:T(2,128)(2,1)S(1)}, u32[]{:S(2)}, u32[]{:S(2)}) async-start(bf16[4,2,131712]{2,1,0:T(2,128)(2,1)} %reshape.140), calls=%async_computation.2 | async-start | bytes 4214784 | tf_op jit(solution)/shard_map/all_to_all | solution.py:75
  311.9 388.7 %all-reduce.4.cloned.1.call-start = ((), (), s32[]{:S(2)}) async-start(), calls=%async_computation.4 | async-start | bytes 38977536 | tf_op jit(solution)/shard_map/psum | solution.py:100
  311.9 13.2 %copy-start.12 = (bf16[1372,768]{1,0:T(8,128)(2,1)S(1)}, bf16[1372,768]{1,0:T(8,128)(2,1)}, u32[]{:S(2)}) copy-start(bf16[1372,768]{1,0:T(8,128)(2,1)} %reshape.126) | copy-start | bytes 6322180
  360.1 5.2 copy-start.10
  360.1 5.2 copy-start.26
  360.1 5.2 copy-start.30
  365.4 11.7 %copy-start.9 = (bf16[28,196,192]{2,1,0:T(8,128)(2,1)S(1)}, bf16[28,196,192]{2,1,0:T(8,128)(2,1)}, u32[]{:S(2)}) copy-start(bf16[28,196,192]{2,1,0:T(8,128)(2,1)} %all_to_all.43) | copy-start | bytes 6322180
  392.1 60.8 %all-to-all-start.3 = ((bf16[28,196,192]{2,0,1:T(8,128)(2,1)}), bf16[28,196,192]{2,0,1:T(8,128)(2,1)}, u32[]{:S(2)}, u32[]{:S(2)}) async-start(bf16[28,196,192]{2,0,1:T(8,128)(2,1)} %copy.77), calls=%async_computation.3 | async-start | bytes 6422528 | tf_op jit(solution)/shard_map/all_to_all | solution.py:97
  459.9 10.8 %copy-start.7 = (bf16[28,196,192]{1,2,0:T(8,128)(2,1)}, bf16[28,196,192]{1,2,0:T(8,128)(2,1)S(1)}, u32[]{:S(2)}) copy-start(bf16[28,196,192]{1,2,0:T(8,128)(2,1)S(1)} %copy.78) | copy-start | bytes 6322180
  478.2 10.5 %copy-start.3 = (bf16[28,49,768]{2,1,0:T(8,128)(2,1)S(1)}, bf16[28,49,768]{2,1,0:T(8,128)(2,1)}, u32[]{:S(2)}) copy-start(bf16[28,49,768]{2,1,0:T(8,128)(2,1)} %param.15) | copy-start | bytes 6322180
  478.2 10.5 %copy-start.14 = (f32[28,49]{1,0:T(8,128)S(1)}, f32[28,49]{1,0:T(8,128)}, u32[]{:S(2)}) copy-start(f32[28,49]{1,0:T(8,128)} %copy-done.13) | copy-start | bytes 16468
  478.2 10.5 %copy-start.20 = (f32[768]{0:T(1024)S(1)}, f32[768]{0:T(1024)}, u32[]{:S(2)}) copy-start(f32[768]{0:T(1024)} %param.17) | copy-start | bytes 9220
  488.5 4.0 copy-start.18
  488.5 4.1 copy-start.16
  488.8 4.9 copy-start.4
  702.3 10.6 %slice-start = ((s8[9437184]{0:T(1024)(128)(4,1)}), s8[4194304]{0:T(1024)(128)(4,1)S(1)}, s32[]{:S(2)}) async-start(s8[9437184]{0:T(1024)(128)(4,1)} %bitcast.89), calls=%async_computation.5 | async-start | bytes 8388608
  704.2 8.8 %slice-start.1 = ((s8[9437184]{0:T(1024)(128)(4,1)}), s8[4194304]{0:T(1024)(128)(4,1)S(1)}, s32[]{:S(2)}) async-start(s8[9437184]{0:T(1024)(128)(4,1)} %bitcast.89), calls=%async_computation.6 | async-start | bytes 8388608
  704.2 8.8 %slice-start.2 = ((s8[9437184]{0:T(1024)(128)(4,1)}), s8[1048576]{0:T(1024)(128)(4,1)S(1)}, s32[]{:S(2)}) async-start(s8[9437184]{0:T(1024)(128)(4,1)} %bitcast.89), calls=%async_computation.7 | async-start | bytes 2097152
  (11 other events, 23.5 us)
Sparse Core Ops, SparseCore 0:
  379.3 321.2 all-reduce.3
where the time goes:
time: 731 us; the launch traced here: 724 us
  waiting for transfers between devices  239 us (33%)
  local copies, waits for them, and re-layouts  220 us (30%)
  matrix products  117 us (16%)
  blocking collectives  73.8 us (10%)
  other arithmetic  44.7 us (6%)
  between operations  15.3 us (2%)
  starting transfers between devices  13.2 us (2%)
    psum x1, waiting for transfers between devices, shards(): lax.psum((grad_gain_one, grad_shift_one, grad_tok_in, grad_tok_inbias, gr...  155 us
    unnamed x86, local copies, waits for them, and re-layouts  71.9 us
    all_to_all x1, waiting for transfers between devices, shards(): lax.all_to_all(grad_columns, 'mix', split_axis=1, concat_axis=2, tiled=True)  55.4 us
    psum x1, blocking collectives, shards(): lax.psum((grad_gain_one, grad_shift_one, grad_tok_in, grad_tok_inbias, gr...  42.5 us
    all_to_all x1, blocking collectives, shards(): lax.all_to_all(normed, 'mix', split_axis=2, concat_axis=1, tiled=True)  31.3 us
    all_to_all x1, waiting for transfers between devices, shards(): lax.all_to_all(mixed_cols, 'mix', split_axis=1, concat_axis=2, tiled=True)  28.5 us
    convert_element_type x4, local copies, waits for them, and re-layouts, shards(): middle = inputs + mixed.astype(jnp.float32)  27.2 us
    convert_element_type x4, local copies, waits for them, and re-layouts, shards(): grad_normed.astype(jnp.float32)  26.3 us
  transfers between devices with their start and end apart: 4, of which 4 were waited for; matrix products, arithmetic and copies ran while one was open for 13% of the time, Pallas kernels for 0%

commit v1 on v0

--- a/solution.py
+++ b/solution.py
@@ -4,6 +4,11 @@
 from jax.sharding import PartitionSpec as P
 
 EPS = 1e-06
+
+
+def copies_bind(chunk):
+    later = jax.lax.psum(jax.lax.psum(chunk, "mix"), "dp")
+    return later
 
 
 def layer_norm(values, gain, shift):
@@ -97,7 +102,7 @@
     grad_normed = lax.all_to_all(grad_columns, "mix", split_axis=1, concat_axis=2, tiled=True)
     grad_inputs, grad_gain_one, grad_shift_one = first_back(grad_normed.astype(jnp.float32))
     patch_grad = (grad_middle + grad_inputs).astype(jnp.bfloat16)
-    summed = lax.psum(
+    summed = copies_bind(
         (
             grad_gain_one,
             grad_shift_one,
@@ -111,8 +116,7 @@
             grad_chan_inbias,
             grad_chan_out,
             grad_chan_outbias,
-        ),
-        ("dp", "mix"),
+        )
     )
     return (
         mixed_out,

time: 731 us -> 1340 us (1.83)
  waiting for transfers between devices: 239 us -> 844 us
    psum x1 -> x2, waiting for transfers between devices: 155 us -> 778 us  [copies_bind(): later = jax.lax.psum(jax.lax.psum(chunk, 'mix'), 'dp')]
    all_to_all x1, waiting for transfers between devices: 55.4 us -> 37 us  [shards(): lax.all_to_all(grad_columns, 'mix', split_axis=1, concat_axis=2, tiled=True)]
    psum x1 -> x2, blocking collectives: 42.5 us -> 51.9 us  [copies_bind(): later = jax.lax.psum(jax.lax.psum(chunk, 'mix'), 'dp')]
  transfers between devices with their start and end apart: 4 -> 5, of which waited for: 4 -> 5; matrix products, arithmetic and copies ran while one was open for 13% -> 7% of each run, Pallas kernels for 0% -> 0%
where the time goes in v1:
time: 1340 us
  waiting for transfers between devices  844 us (63%)
  local copies, waits for them, and re-layouts  219 us (16%)
  matrix products  117 us (9%)
  blocking collectives  83.2 us (6%)
  other arithmetic  44.8 us (3%)
  between operations  15.4 us (1%)
    psum x2, waiting for transfers between devices, copies_bind(): later = jax.lax.psum(jax.lax.psum(chunk, 'mix'), 'dp')  778 us
    unnamed x86, local copies, waits for them, and re-layouts  70.8 us
    psum x2, blocking collectives, copies_bind(): later = jax.lax.psum(jax.lax.psum(chunk, 'mix'), 'dp')  51.9 us
    all_to_all x1, waiting for transfers between devices, shards(): lax.all_to_all(grad_columns, 'mix', split_axis=1, concat_axis=2, tiled=True)  37 us
    all_to_all x1, blocking collectives, shards(): lax.all_to_all(normed, 'mix', split_axis=2, concat_axis=1, tiled=True)  31.3 us
    all_to_all x1, waiting for transfers between devices, shards(): lax.all_to_all(mixed_cols, 'mix', split_axis=1, concat_axis=2, tiled=True)  28.5 us
    convert_element_type x4, local copies, waits for them, and re-layouts, shards(): middle = inputs + mixed.astype(jnp.float32)  27.2 us
  transfers between devices with their start and end apart: 5, of which 5 were waited for; matrix products, arithmetic and copies ran while one was open for 7% of the time, Pallas kernels for 0%

profile of v1, /device:TPU:0, one launch (start us, length us, event | category | flops | bytes accessed | tf_op | source)
XLA Modules:
  0.0 1336.3 jit_solution(11456076228916010979)
XLA Ops:
  15.3 11.4 copy.67
  26.7 11.5 reshape.138
  38.2 31.3 %all_to_all.54 = bf16[4,2,131712]{2,1,0:T(2,128)(2,1)} all-to-all(bf16[4,2,131712]{2,1,0:T(2,128)(2,1)} %reshape.138), channel_id=1, replica_groups=mesh['dp'=8,'mix'=4] {'mix'}, dimensions={0} | all-to-all | bytes 4214784 | tf_op jit(solution)/shard_map/all_to_all | solution.py:42
  69.6 11.9 reshape.139
  81.5 9.6 copy.68
  96.9 7.8 fusion.17
  109.8 7.4 copy.70
  131.2 28.5 %all-to-all-done.1 = bf16[28,196,192]{2,0,1:T(8,128)(2,1)} async-done(((bf16[28,196,192]{2,0,1:T(8,128)(2,1)}), bf16[28,196,192]{2,0,1:T(8,128)(2,1)}, u32[]{:S(2)}, u32[]{:S(2)}) %all-to-all-start.1) | async-done | bytes 2107424 | tf_op jit(solution)/shard_map/all_to_all | solution.py:52
  159.7 7.5 copy.71
  179.2 7.5 copy.73
  186.7 7.7 reshape.130
  202.5 17.7 %multiply_convert_fusion = (bf16[1372,3072]{1,0:T(8,128)(2,1)}, f32[1372,3072]{1,0:T(8,128)}) fusion(f32[3072]{0:T(1024)S(1)} %copy-done.27, bf16[1372,768]{1,0:T(8,128)(2,1)} %reshape.126, bf16[768,3072]{1,0:T(8,128)(2,1)} %param.25), kind=kOutput, calls=%fused_computation.10 | convolution fusion | flops 6516056064 | bytes 32126976 | tf_op jit(solution)/shard_map/dot_general | solution.py:56
  220.2 19.9 %convert_reduce_fusion = (f32[3072]{0:T(1024)S(1)}, bf16[1372,3072]{1,0:T(8,128)(2,1)S(1)}) fusion(f32[1372,3072]{1,0:T(8,128)} %get-tuple-element.52, f32[3072]{0:T(1024)S(1)} %copy-done.27, bf16[1372,768]{1,0:T(8,128)(2,1)S(1)} %copy-done.11, bf16[3072,768]{1,0:T(8,128)(2,1)} %param.27), kind=kOutput, calls=%fused_computation.9 | convolution fusion | flops 6570845184 | bytes 32139264 | tf_op jit(solution)/shard_map/rc,fc->rf/dot_general | solution.py:71
  240.2 8.3 fusion.41
  258.4 12.2 convolution_add_fusion
  275.8 7.4 fusion.39
  286.0 10.8 copy.74
  296.8 11.5 reshape.140
  312.0 13.2 fusion.43
  325.2 12.2 fusion.42
  337.7 10.9 reshape.141
  348.7 8.6 copy.75
  365.5 9.6 convert_reduce_fusion.1
  379.2 336.4 %all-reduce.9.cloned.1.call-done = (f32[196,384]{1,0:T(8,128)}, f32[384,196]{0,1:T(8,128)}, f32[768,3072]{1,0:T(8,128)}, f32[3072,768]{1,0:T(8,128)}) async-done(((f32[196,384]{1,0:T(8,128)}, f32[384,196]{0,1:T(8,128)}, f32[768,3072]{1,0:T(8,128)}, f32[3072,768]{1,0:T(8,128)}), (f32[196,384]{1,0:T(8,128)}, f32[384,196]{0,1:T(8,128)}, f32[768,3072]{1,0:T(8,128)}, ...) | async-done | bytes 19476496 | tf_op jit(solution)/shard_map/psum | solution.py:10
  720.9 7.5 copy.77
  733.8 37.0 %all-to-all-done.3 = bf16[28,196,192]{2,0,1:T(8,128)(2,1)} async-done(((bf16[28,196,192]{2,0,1:T(8,128)(2,1)}), bf16[28,196,192]{2,0,1:T(8,128)(2,1)}, u32[]{:S(2)}, u32[]{:S(2)}) %all-to-all-start.3) | async-done | bytes 2107424 | tf_op jit(solution)/shard_map/all_to_all | solution.py:102
  788.5 7.6 copy.80
  796.1 7.8 reshape.131
  813.0 11.3 all-reduce.2
  824.3 40.5 %all-reduce = (f32[768]{0:T(1024)}, f32[768]{0:T(1024)}, f32[384]{0:T(512)}, f32[196]{0:T(256)}, f32[768]{0:T(1024)}, /*index=5*/f32[768]{0:T(1024)}, f32[3072]{0:T(1024)}, f32[768]{0:T(1024)}) all-reduce(f32[768]{0:T(1024)S(1)} %get-tuple-element.30, f32[768]{0:T(1024)S(1)} %get-tuple-element.31, ...), channel_id=1, replica_groups=mesh['dp'=8,'mix'=4] {'dp'}, use_global_device_ids=true, to_apply=%region_10.11 | all-reduce | flops 7492 | bytes 59936 | tf_op jit(solution)/shard_map/psum | solution.py:10
  871.6 441.5 %all-reduce.7.cloned.1.call-done = (f32[196,384]{1,0:T(8,128)}, f32[384,196]{0,1:T(8,128)}, f32[768,3072]{1,0:T(8,128)}, f32[3072,768]{1,0:T(8,128)}) async-done(((f32[196,384]{1,0:T(8,128)}, f32[384,196]{0,1:T(8,128)}, f32[768,3072]{1,0:T(8,128)}, f32[3072,768]{1,0:T(8,128)}), (f32[196,384]{1,0:T(8,128)}, f32[384,196]{0,1:T(8,128)}, f32[768,3072]{1,0:T(8,128)}, ...) | async-done | bytes 19476496 | tf_op jit(solution)/shard_map/psum | solution.py:10
  1316.7 8.8 copy.99
  (134 shorter events, 138.0 us)
Async XLA Ops:
  7.2 89.7 %copy-start = (bf16[196,384]{1,0:T(8,128)(2,1)S(1)}, bf16[196,384]{1,0:T(8,128)(2,1)}, u32[]{:S(2)}) copy-start(bf16[196,384]{1,0:T(8,128)(2,1)} %param.19) | copy-start | bytes 451588
  7.2 6.0 copy-start.2
  7.2 6.0 copy-start.19
  7.2 6.0 copy-start.23
  91.1 5.8 copy-start.29
  96.8 9.8 copy-start.25
  96.9 9.8 copy-start.31
  117.1 42.5 %all-to-all-start.1 = ((bf16[28,196,192]{2,0,1:T(8,128)(2,1)}), bf16[28,196,192]{2,0,1:T(8,128)(2,1)}, u32[]{:S(2)}, u32[]{:S(2)}) async-start(bf16[28,196,192]{2,0,1:T(8,128)(2,1)} %copy.70), calls=%async_computation.1 | async-start | bytes 6422528 | tf_op jit(solution)/shard_map/all_to_all | solution.py:52
  202.5 17.7 %copy-start.11 = (bf16[1372,768]{1,0:T(8,128)(2,1)S(1)}, bf16[1372,768]{1,0:T(8,128)(2,1)}, u32[]{:S(2)}) copy-start(bf16[1372,768]{1,0:T(8,128)(2,1)} %reshape.128) | copy-start | bytes 6322180
  202.5 37.7 %slice-start.3 = ((s8[4718592]{0:T(1024)(128)(4,1)}), s8[4194304]{0:T(1024)(128)(4,1)S(1)}, s32[]{:S(2)}) async-start(s8[4718592]{0:T(1024)(128)(4,1)} %bitcast.91), calls=%async_computation.9 | async-start | bytes 8388608
  220.2 20.0 %slice-start.4 = ((s8[4718592]{0:T(1024)(128)(4,1)}), s8[524288]{0:T(1024)(128)(4,1)S(1)}, s32[]{:S(2)}) async-start(s8[4718592]{0:T(1024)(128)(4,1)} %bitcast.91), calls=%async_computation.10 | async-start | bytes 1048576
  240.2 8.4 copy-start.33
  253.7 4.7 copy-start.28
  275.8 9.6 copy-start.6
  308.4 29.4 %all-to-all-start.2 = ((bf16[4,2,131712]{2,1,0:T(2,128)(2,1)}), bf16[4,2,131712]{2,1,0:T(2,128)(2,1)S(1)}, u32[]{:S(2)}, u32[]{:S(2)}) async-start(bf16[4,2,131712]{2,1,0:T(2,128)(2,1)} %reshape.140), calls=%async_computation.2 | async-start | bytes 4214784 | tf_op jit(solution)/shard_map/all_to_all | solution.py:80
  312.0 403.6 %all-reduce.9.cloned.1.call-start = ((), (), s32[]{:S(2)}) async-start(), calls=%async_computation.5 | async-start | bytes 38977536 | tf_op jit(solution)/shard_map/psum | solution.py:10
  312.0 13.2 copy-start.12
  360.2 5.2 copy-start.10
  360.2 5.2 copy-start.26
  360.2 5.3 copy-start.30
  365.4 11.5 copy-start.9
  379.1 934.0 %all-reduce.7.cloned.1.call-start = ((), (), s32[]{:S(2)}) async-start(), calls=%async_computation.4 | async-start | bytes 38977536 | tf_op jit(solution)/shard_map/psum | solution.py:10
  728.4 42.4 %all-to-all-start.3 = ((bf16[28,196,192]{2,0,1:T(8,128)(2,1)}), bf16[28,196,192]{2,0,1:T(8,128)(2,1)}, u32[]{:S(2)}, u32[]{:S(2)}) async-start(bf16[28,196,192]{2,0,1:T(8,128)(2,1)} %copy.77), calls=%async_computation.3 | async-start | bytes 6422528 | tf_op jit(solution)/shard_map/all_to_all | solution.py:102
  777.8 10.8 copy-start.7
  796.1 10.4 copy-start.3
  796.1 10.4 copy-start.14
  796.1 10.4 copy-start.20
  806.2 4.1 copy-start.18
  806.2 4.1 copy-start.16
  1314.8 10.6 slice-start
  1316.7 8.8 slice-start.1
  1316.7 8.8 slice-start.2
  (12 other events, 26.5 us)
Sparse Core Ops, SparseCore 0:
  379.3 336.2 all-reduce.8
  721.2 591.8 all-reduce.6
